TPU v7x, 32 devices: a whole 2x2x4 slice. The times are simulated.
32 devices in a mesh: rep: 1, ep: 32 (over z, y, x, core), hid: 1.
Axes of the slice: x: 2, y: 2, z: 4, core: 2. Of those that a mesh axis runs over, the one named last changes fastest.
Arguments:
- tokens: bfloat16 [4096, 2048], P(('rep', 'ep')), may hold values from -6 to 6
- cotangent: bfloat16 [4096, 2048], P(('rep', 'ep')), may hold values from -2 to 2
- routing: float32 [4096, 8], P(('rep', 'ep')), may hold values from 0.05 to 0.5
- expert_ids: int32 [4096, 8], P(('rep', 'ep')), may hold values from 0 to 63, all different within a row; in each aligned block of 128 rows (0 to 127, 128 to 255, ...) at most 20 rows name the same one
- gate_weight: bfloat16 [64, 2048, 768], P('ep', None, 'hid'), may hold values from -0.125 to 0.125
- up_weight: bfloat16 [64, 2048, 768], P('ep', None, 'hid'), may hold values from -0.125 to 0.125
- down_weight: bfloat16 [64, 768, 2048], P('ep', 'hid'), may hold values from -0.21875 to 0.21875
Outputs:
- input_grad: float32 [4096, 2048], P(('rep', 'ep'), 'hid')
- gate_grad: float32 [4096, 8], P(('rep', 'ep'))
Inputs may be any that keep to these rules, and one draw needn't show every extreme that they name: `expert_ids`: among the 128 tokens of one index of ep (aligned blocks of rows), no expert is picked more than 20 times, a bound that some block reaches; the 8 picks of a token are different experts.
All inputs are finite; a program needn't handle non-finite values.
Results may differ from a plain program's by a relative error of at most 0.0029.
Values may be sent and summed in bfloat16 or wider, within the bound.
A program may use at most 128 MiB of HBM per device.

v0:
```python
import jax
import jax.numpy as jnp
from jax import lax
from jax.sharding import PartitionSpec as P


def slot_rank(flat, experts):
    onehot = (flat[:, None] == jnp.arange(experts, dtype=jnp.int32)[None, :]).astype(jnp.int32)
    before = jnp.cumsum(onehot, axis=0) - onehot
    return jnp.sum(before * onehot, axis=1)


def expert_math(inputs, grads_in, w_gate, w_upper, w_down, w_joined):
    gate_pre = jnp.einsum("erd,edf->erf", inputs, w_gate, preferred_element_type=jnp.float32)
    up_pre = jnp.einsum("erd,edf->erf", inputs, w_upper, preferred_element_type=jnp.float32)
    upward = jnp.einsum("erd,efd->erf", grads_in, w_down, preferred_element_type=jnp.float32)
    sigma = jax.nn.sigmoid(gate_pre)
    silu_val = gate_pre * sigma
    hidden = silu_val * up_pre
    pick_gate = jnp.sum(hidden * upward, axis=2)
    gate_delta = (upward * up_pre * sigma * (1.0 + gate_pre * (1.0 - sigma))).astype(jnp.bfloat16)
    up_delta = (upward * silu_val).astype(jnp.bfloat16)
    deltas = jnp.concatenate([gate_delta, up_delta], axis=2)
    partial_value = jnp.einsum("erf,edf->erd", deltas, w_joined, preferred_element_type=jnp.float32)
    return (partial_value, pick_gate)


def combine_rows(returned, dest, token_of, routing, tok_rows):
    slots_all = returned.shape[0]
    mixing = (
        jnp.zeros((tok_rows, slots_all), jnp.float32).at[token_of, dest].set(routing.reshape(-1))
    )
    return jnp.dot(
        mixing, returned, precision=lax.Precision.HIGHEST, preferred_element_type=jnp.float32
    )


def local(tokens, cotangent, routing, expert_ids, gate_weight, up_weight, down_weight):
    count_ep = lax.axis_size("ep")
    local_experts = gate_weight.shape[0]
    experts = local_experts * count_ep
    tok_rows, top_picks = expert_ids.shape
    width = tokens.shape[1]
    capacity = 5 * tok_rows * top_picks // (4 * experts)
    flat = expert_ids.reshape(-1)
    dest = flat * capacity + slot_rank(flat, experts)
    token_of = jnp.arange(tok_rows * top_picks, dtype=jnp.int32) // top_picks
    slot_token = jnp.full((experts * capacity,), tok_rows, jnp.int32).at[dest].set(token_of)
    padding = jnp.zeros((1, width), tokens.dtype)
    bucket_shape = (count_ep, local_experts, capacity, width)
    token_rows = jnp.concatenate([tokens, padding], 0)[slot_token].reshape(bucket_shape)
    cotan_rows = jnp.concatenate([cotangent, padding], 0)[slot_token].reshape(bucket_shape)
    joined_weight = jnp.concatenate([gate_weight, up_weight], axis=2)
    inputs = lax.all_to_all(token_rows, "ep", split_axis=0, concat_axis=0, tiled=True)
    grads_in = lax.all_to_all(cotan_rows, "ep", split_axis=0, concat_axis=0, tiled=True)
    sources, owned, slots, row_width = inputs.shape
    inputs = inputs.transpose(1, 0, 2, 3).reshape(owned, sources * slots, row_width)
    grads_in = grads_in.transpose(1, 0, 2, 3).reshape(owned, sources * slots, row_width)
    partial_value, pick_gate = expert_math(
        inputs, grads_in, gate_weight, up_weight, down_weight, joined_weight
    )
    pick_gate = pick_gate.reshape(owned, sources, slots)
    partial_value = partial_value.reshape(owned, sources, slots, row_width).transpose(1, 0, 2, 3)
    returned = lax.all_to_all(partial_value, "ep", split_axis=0, concat_axis=0, tiled=True)
    gate_back = lax.all_to_all(
        pick_gate.transpose(1, 0, 2), "ep", split_axis=0, concat_axis=0, tiled=True
    )
    returned = returned.reshape(experts * capacity, returned.shape[3])
    weighted = combine_rows(returned, dest, token_of, routing, tok_rows)
    gate_grad = gate_back.reshape(-1)[dest].reshape(tok_rows, top_picks)
    input_grad = lax.psum_scatter(weighted, "hid", scatter_dimension=1, tiled=True)
    gate_total = lax.psum(gate_grad, "hid")
    return (input_grad, gate_total)


def solution(mesh):
    placed = (
        P(("rep", "ep"), None),
        P(("rep", "ep"), None),
        P(("rep", "ep"), None),
        P(("rep", "ep"), None),
        P("ep", None, "hid"),
        P("ep", None, "hid"),
        P("ep", "hid", None),
    )
    return jax.shard_map(
        local,
        mesh=mesh,
        in_specs=placed,
        out_specs=(P(("rep", "ep"), "hid"), P(("rep", "ep"), None)),
        check_vma=False,
    )
```

profile of v0, /device:TPU:0, one launch (start us, length us, event | category | flops | bytes accessed | tf_op | source)
XLA Modules:
  0.0 629.3 jit_solution(10250468809868440312)
XLA Ops:
  2.3 18.0 %reduce-window.6 = s32[64,8,128]{2,1,0:T(8,128)S(1)} reduce-window(s32[64,8,128]{2,1,0:T(8,128)S(1)} %fusion.19, s32[]{:T(128)} %constant.34.clone.1), window={size=1x1x128 pad=0_0x0_0x127_0}, to_apply=%region_0.0 | reduce-window | flops 8323072 | bytes 524292 | tf_op jit(solution)/shard_map/reduce-window
  21.2 4.3 scatter_custom_fusion
  26.6 6.2 gather_fusion.1
  32.8 8.9 %reshape.127 = bf16[32,2,20,2048]{3,2,1,0:T(8,128)(2,1)} reshape(bf16[1280,2048]{1,0:T(8,128)(2,1)} %gather_fusion.1) | data formatting | bytes 10485760 | tf_op jit(solution)/shard_map/reshape | solution.py:51
  41.8 11.1 %copy.34 = bf16[32,2,20,2048]{3,1,2,0:T(2,128)(2,1)} copy(bf16[32,2,20,2048]{3,2,1,0:T(8,128)(2,1)} %reshape.127) | data formatting | bytes 10485760 | tf_op jit(solution)/shard_map/reshape | solution.py:51
  52.9 7.4 %all-to-all-start.1 = ((bf16[32,2,20,2048]{3,1,2,0:T(2,128)(2,1)}), bf16[32,2,20,2048]{3,1,2,0:T(2,128)(2,1)}, u32[]{:S(2)}, u32[]{:S(2)}) async-start(bf16[32,2,20,2048]{3,1,2,0:T(2,128)(2,1)} %copy.34), calls=%async_computation.1 | async-start | bytes 10485760 | tf_op jit(solution)/shard_map/all_to_all | solution.py:54
  60.4 6.1 gather_fusion
  66.5 8.9 %reshape.125 = bf16[32,2,20,2048]{3,2,1,0:T(8,128)(2,1)} reshape(bf16[1280,2048]{1,0:T(8,128)(2,1)} %gather_fusion) | data formatting | bytes 10485760 | tf_op jit(solution)/shard_map/reshape | solution.py:52
  75.4 11.1 %copy.32 = bf16[32,2,20,2048]{3,1,2,0:T(2,128)(2,1)} copy(bf16[32,2,20,2048]{3,2,1,0:T(8,128)(2,1)} %reshape.125) | data formatting | bytes 10485760 | tf_op jit(solution)/shard_map/reshape | solution.py:52
  86.6 90.2 %all-to-all-done.1 = bf16[32,2,20,2048]{3,1,2,0:T(2,128)(2,1)} async-done(((bf16[32,2,20,2048]{3,1,2,0:T(2,128)(2,1)}), bf16[32,2,20,2048]{3,1,2,0:T(2,128)(2,1)}, u32[]{:S(2)}, u32[]{:S(2)}) %all-to-all-start.1) | async-done | bytes 5242912 | tf_op jit(solution)/shard_map/all_to_all | solution.py:54
  176.8 4.0 all-to-all-start
  180.9 11.3 %fusion.6 = f32[2,640,768]{2,1,0:T(8,128)} fusion(bf16[2,2048,768]{2,1,0:T(8,128)(2,1)} %param.11, bf16[2,640,2048]{2,0,1:T(2,128)(2,1)} %bitcast.7), kind=kOutput, calls=%fused_computation.11 | convolution fusion | flops 4026531840 | bytes 15466496 | tf_op jit(solution)/shard_map/erd,edf->erf/dot_general | solution.py:14
  192.2 11.2 %fusion.8 = f32[2,640,768]{2,1,0:T(8,128)} fusion(bf16[2,2048,768]{2,1,0:T(8,128)(2,1)} %param.12, bf16[2,640,2048]{2,0,1:T(2,128)(2,1)} %bitcast.7), kind=kOutput, calls=%fused_computation.13 | convolution fusion | flops 4026531840 | bytes 15466496 | tf_op jit(solution)/shard_map/erd,edf->erf/dot_general | solution.py:15
  203.4 93.8 %all-to-all-done = bf16[32,2,20,2048]{3,1,2,0:T(2,128)(2,1)} async-done(((bf16[32,2,20,2048]{3,1,2,0:T(2,128)(2,1)}), bf16[32,2,20,2048]{3,1,2,0:T(2,128)(2,1)}, u32[]{:S(2)}, u32[]{:S(2)}) %all-to-all-start) | async-done | bytes 5242912 | tf_op jit(solution)/shard_map/all_to_all | solution.py:55
  297.2 15.1 %multiply_reduce_fusion = (f32[2,640]{1,0:T(2,128)S(1)}, bf16[2,640,768]{2,1,0:T(8,128)(2,1)S(1)}, bf16[2,640,768]{2,1,0:T(8,128)(2,1)}) fusion(f32[2,640,768]{2,1,0:T(8,128)} %fusion.8, f32[2,640,768]{2,1,0:T(8,128)} %fusion.6, bf16[2,768,2048]{2,1,0:T(8,128)(2,1)} %param.13, bf16[2,640,2048]{2,0,1:T(2,128)(2,1)} %bitcast.5), kind=kOutput, calls=%fused_computation.18 | convolution fusion | flops 4042259200 | bytes 23335936 | tf_op jit(solution)/shard_map/erd,efd->erf/dot_general | solution.py:16
  316.8 14.3 %fusion = f32[2,640,2048]{2,1,0:T(8,128)} fusion(bf16[2,2048,768]{2,1,0:T(8,128)(2,1)} %param.12, bf16[2,2048,768]{2,1,0:T(8,128)(2,1)} %param.11, bf16[2,640,768]{2,1,0:T(8,128)(2,1)} %get-tuple-element.8, bf16[2,640,768]{2,1,0:T(8,128)(2,1)S(1)} %get-tuple-element.7), kind=kOutput, calls=%fused_computation.5 | convolution fusion | flops 8086093824 | bytes 27000832 | tf_op jit(solution)/shard_map/erf,edf->erd/dot_general | solution.py:24
  331.2 18.7 %copy.37 = f32[2,640,2048]{2,0,1:T(2,128)} copy(f32[2,640,2048]{2,1,0:T(8,128)} %fusion) | data formatting | bytes 20971520 | tf_op jit(solution)/shard_map/erf,edf->erd/dot_general | solution.py:24
  349.9 6.0 all-to-all-start.2
  356.3 4.5 scatter_custom_fusion.1
  361.0 6.6 %gather_fusion.2 = f32[1024]{0:T(1024)S(1)} fusion(f32[1280]{0:T(1024)S(1)} %reshape.132, s32[1024]{0:T(1024)S(1)} %broadcast_clamp_fusion), kind=kCustom, calls=%fused_computation.2 | custom fusion | bytes 12288 | tf_op jit(solution)/shard_map/gather | solution.py:70
  368.3 219.5 %all-to-all-done.2 = f32[32,2,20,2048]{3,1,2,0:T(2,128)} async-done(((f32[32,2,20,2048]{3,1,2,0:T(2,128)}), f32[32,2,20,2048]{3,1,2,0:T(2,128)}, u32[]{:S(2)}, u32[]{:S(2)}) %all-to-all-start.2) | async-done | bytes 10485792 | tf_op jit(solution)/shard_map/all_to_all | solution.py:64
  587.8 17.8 %copy.38 = f32[32,2,20,2048]{3,2,1,0:T(8,128)} copy(f32[32,2,20,2048]{3,1,2,0:T(2,128)} %all-to-all-done.2) | data formatting | bytes 20971520 | tf_op jit(solution)/shard_map/all_to_all | solution.py:64
  605.7 12.9 %reshape.130 = f32[1280,2048]{1,0:T(8,128)} reshape(f32[32,2,20,2048]{3,2,1,0:T(8,128)} %copy.38) | data formatting | bytes 20971520 | tf_op jit(solution)/shard_map/reshape | solution.py:68
  618.5 10.6 %fusion.26 = f32[128,2048]{1,0:T(8,128)} fusion(f32[128,1280]{1,0:T(8,128)S(1)} %reshape.137, f32[1280,2048]{1,0:T(8,128)} %reshape.130), kind=kOutput, calls=%fused_computation.57 | convolution fusion | flops 4026531840 | bytes 12189696 | tf_op jit(solution)/shard_map/dot_general | solution.py:33
  (42 shorter events, 9.5 us)
Async XLA Ops:
  52.9 7.5 %copy-start = (bf16[128,2048]{1,0:T(8,128)(2,1)S(1)}, bf16[128,2048]{1,0:T(8,128)(2,1)}, u32[]{:S(2)}) copy-start(bf16[128,2048]{1,0:T(8,128)(2,1)} %param.8) | copy-start | bytes 1572868
  52.9 123.9 %all-to-all-start.1 = ((bf16[32,2,20,2048]{3,1,2,0:T(2,128)(2,1)}), bf16[32,2,20,2048]{3,1,2,0:T(2,128)(2,1)}, u32[]{:S(2)}, u32[]{:S(2)}) async-start(bf16[32,2,20,2048]{3,1,2,0:T(2,128)(2,1)} %copy.34), calls=%async_computation.1 | async-start | bytes 10485760 | tf_op jit(solution)/shard_map/all_to_all | solution.py:54
  176.8 120.4 %all-to-all-start = ((bf16[32,2,20,2048]{3,1,2,0:T(2,128)(2,1)}), bf16[32,2,20,2048]{3,1,2,0:T(2,128)(2,1)}, u32[]{:S(2)}, u32[]{:S(2)}) async-start(bf16[32,2,20,2048]{3,1,2,0:T(2,128)(2,1)} %copy.32), calls=%async_computation | async-start | bytes 10485760 | tf_op jit(solution)/shard_map/all_to_all | solution.py:55
  313.1 36.8 %all-to-all-start.3 = ((f32[32,2,20]{2,1,0:T(2,128)}), f32[32,2,20]{2,1,0:T(2,128)S(1)}, u32[]{:S(2)}, u32[]{:S(2)}) async-start(f32[32,2,20]{2,1,0:T(2,128)} %copy.39), calls=%async_computation.3 | async-start | bytes 65536 | tf_op jit(solution)/shard_map/all_to_all | solution.py:65
  349.9 6.0 copy-start.1
  349.9 6.2 copy-start.3
  349.9 6.3 copy-start.2
  349.9 237.9 %all-to-all-start.2 = ((f32[32,2,20,2048]{3,1,2,0:T(2,128)}), f32[32,2,20,2048]{3,1,2,0:T(2,128)}, u32[]{:S(2)}, u32[]{:S(2)}) async-start(f32[32,2,20,2048]{3,1,2,0:T(2,128)} %bitcast.35), calls=%async_computation.2 | async-start | bytes 20971520 | tf_op jit(solution)/shard_map/all_to_all | solution.py:64
where the time goes:
time: 636 us; the launch traced here: 629 us
  waiting for transfers between devices  404 us (64%)
  local copies, waits for them, and re-layouts  122 us (19%)
  matrix products  62.6 us (10%)
  starting transfers between devices  21.2 us (3%)
  other arithmetic  19.2 us (3%)
    all_to_all x1, waiting for transfers between devices, local(): lax.all_to_all(partial_value, 'ep', split_axis=0, concat_axis=0, tiled=True)  219 us
    all_to_all x1, waiting for transfers between devices, local(): lax.all_to_all(cotan_rows, 'ep', split_axis=0, concat_axis=0, tiled=True)  93.8 us
    all_to_all x1, waiting for transfers between devices, local(): lax.all_to_all(token_rows, 'ep', split_axis=0, concat_axis=0, tiled=True)  90.2 us
    reshape x2, local copies, waits for them, and re-layouts, local(): jnp.concatenate([cotangent, padding], 0)[slot_token].reshape(bucket_shape)  20.1 us
    reshape x2, local copies, waits for them, and re-layouts, local(): jnp.concatenate([tokens, padding], 0)[slot_token].reshape(bucket_shape)  20 us
    dot_general x1, local copies, waits for them, and re-layouts, expert_math(): jnp.einsum('erf,edf->erd', deltas, w_joined, preferred_element_type=jnp.f...  18.7 us
    another operation x3, other arithmetic  18.2 us
    all_to_all x1, local copies, waits for them, and re-layouts, local(): lax.all_to_all(partial_value, 'ep', split_axis=0, concat_axis=0, tiled=True)  17.8 us
  transfers between devices with their start and end apart: 4, of which 3 were waited for; matrix products, arithmetic and copies ran while one was open for 15% of the time, Pallas kernels for 0%

commit v1 on v0

v1 whole, which is shorter than its diff:
```python
import jax
import jax.numpy as jnp
from jax import lax
from jax.sharding import PartitionSpec as P

BF = jnp.bfloat16
F32 = jnp.float32


def dot(a, b):
    return jnp.dot(a, b, preferred_element_type=F32)


def split_two(value):
    high = lax.reduce_precision(value, 8, 7)
    return high.astype(BF), (value - high).astype(BF)


def local(tokens, cotangent, routing, expert_ids, gate_weight, up_weight, down_weight):
    count = lax.axis_size("ep")
    owned = gate_weight.shape[0]
    experts = owned * count
    tok_rows, top = expert_ids.shape
    width = tokens.shape[1]
    cap = 5 * tok_rows * top // (4 * experts)
    slots = experts * cap

    onehot = expert_ids[:, :, None] == jnp.arange(experts, dtype=jnp.int32)[None, None, :]
    picked = jnp.any(onehot, axis=1)
    row = jnp.arange(tok_rows, dtype=jnp.int32)
    lower = (row[:, None] > row[None, :]).astype(BF)
    before = dot(lower, picked.astype(BF))
    rank = jnp.where(picked, before, -1.0).astype(BF)
    slot = jnp.arange(slots, dtype=jnp.int32)
    spread = (slot[:, None] // cap == jnp.arange(experts, dtype=jnp.int32)[None, :]).astype(BF)
    place = (slot % cap).astype(F32)
    rank_of = lax.dot_general(spread, rank, (((1,), (1,)), ((), ())), preferred_element_type=F32)
    choose = (rank_of == place[:, None]).astype(BF)
    rank_back = lax.dot_general(rank, spread, (((1,), (1,)), ((), ())), preferred_element_type=F32)
    choose_back = rank_back == place[None, :]

    def exchange(value):
        return lax.all_to_all(value, "ep", split_axis=0, concat_axis=0, tiled=True)

    def by_expert(value):
        value = value.reshape(count, owned, cap, value.shape[1])
        return value.transpose(1, 0, 2, 3).reshape(owned, count * cap, value.shape[3])

    def by_source(value):
        value = value.reshape(owned, count, cap, value.shape[2])
        return value.transpose(1, 0, 2, 3).reshape(slots, value.shape[3])

    inputs = by_expert(exchange(dot(choose, tokens).astype(BF)))
    grads_in = by_expert(exchange(dot(choose, cotangent).astype(BF)))
    gate_pre = jnp.einsum("erd,edf->erf", inputs, gate_weight, preferred_element_type=F32)
    up_pre = jnp.einsum("erd,edf->erf", inputs, up_weight, preferred_element_type=F32)
    upward = jnp.einsum("erd,efd->erf", grads_in, down_weight, preferred_element_type=F32)
    sigma = jax.nn.sigmoid(gate_pre)
    silu_val = gate_pre * sigma
    pick_gate = jnp.sum(silu_val * up_pre * upward, axis=2, keepdims=True)
    gate_delta = (upward * up_pre * sigma * (1.0 + gate_pre * (1.0 - sigma))).astype(BF)
    up_delta = (upward * silu_val).astype(BF)
    deltas = jnp.concatenate([gate_delta, up_delta], axis=2)
    joined = jnp.concatenate([gate_weight, up_weight], axis=2)

    half = width // 2
    gate_high, gate_low = split_two(pick_gate)
    lane = jnp.arange(128, dtype=jnp.int32)[None, None, :]
    gate_cols = jnp.where(lane == 0, gate_high, jnp.where(lane == 1, gate_low, jnp.zeros((), BF)))
    first = jnp.einsum("erf,edf->erd", deltas, joined[:, :half], preferred_element_type=F32).astype(BF)
    second = jnp.einsum("erf,edf->erd", deltas, joined[:, half:], preferred_element_type=F32).astype(BF)
    back_a = exchange(by_source(jnp.concatenate([first, gate_cols], axis=2)))
    back_b = exchange(by_source(second))

    amount = jnp.sum(jnp.where(onehot, routing[:, :, None], 0.0), axis=1)
    amount_high, amount_low = split_two(amount)
    zero = jnp.zeros((), BF)

    def mix(part):
        wide = lax.dot_general(part, spread, (((1,), (1,)), ((), ())), preferred_element_type=F32)
        return jnp.where(choose_back, wide.astype(BF), zero)

    mixing = jnp.concatenate([mix(amount_high), mix(amount_low)], axis=0)

    def combine(value):
        both = dot(mixing, value)
        return both[:tok_rows] + both[tok_rows:]

    weighted = jnp.concatenate([combine(back_a[:, :half]), combine(back_b)], axis=1)
    gates = back_a[:, half:half + 2].T

    def gate_part(i):
        return dot(jnp.where(choose_back, gates[i][None, :], zero), spread)

    gate_sum = gate_part(0) + gate_part(1)
    gate_grad = jnp.sum(jnp.where(onehot, gate_sum[:, None, :], 0.0), axis=2)
    input_grad = lax.psum_scatter(weighted, "hid", scatter_dimension=1, tiled=True)
    return (input_grad, lax.psum(gate_grad, "hid"))


def solution(mesh):
    placed = (
        P(("rep", "ep"), None),
        P(("rep", "ep"), None),
        P(("rep", "ep"), None),
        P(("rep", "ep"), None),
        P("ep", None, "hid"),
        P("ep", None, "hid"),
        P("ep", "hid", None),
    )
    return jax.shard_map(
        local,
        mesh=mesh,
        in_specs=placed,
        out_specs=(P(("rep", "ep"), "hid"), P(("rep", "ep"), None)),
        check_vma=False,
    )
```

time: 636 us -> 442 us (0.69)
  waiting for transfers between devices: 404 us -> 289 us
  local copies, waits for them, and re-layouts: 122 us -> 59.7 us
  other arithmetic: 19.2 us -> 3.31 us
    all_to_all x4, waiting for transfers between devices: 404 us -> 289 us  [exchange(): return lax.all_to_all(value, 'ep', split_axis=0, concat_axis=0, tiled=True)]
    reshape x9 -> x0, local copies, waits for them, and re-layouts: 53.4 us -> none  [the longest x2 20.1 us: local(): jnp.concatenate([cotangent, padding], 0)[slot_token].reshape(bucket_shape)]
    transpose x1 -> x5, local copies, waits for them, and re-layouts: 0.64 us -> 22.8 us  [the longest x2 21 us: by_expert(): value.transpose(1, 0, 2, 3).reshape(owned, count * cap, value.shape[3])]
    gather x3 -> x0, local copies, waits for them, and re-layouts: 18.9 us -> none  [the longest x1 6.56 us: local(): gate_grad = gate_back.reshape(-1)[dest].reshape(tok_rows, top_picks)]
    dot_general x1 -> x0, local copies, waits for them, and re-layouts: 18.7 us -> none  [expert_math(): jnp.einsum('erf,edf->erd', deltas, w_joined, preferred_element_type=jnp.f...]
    another operation x3 -> x0, other arithmetic: 18.2 us -> none
    all_to_all x1 -> x4, local copies, waits for them, and re-layouts: 17.8 us -> 24.6 us  [exchange(): return lax.all_to_all(value, 'ep', split_axis=0, concat_axis=0, tiled=True)]
    dot_general x5 -> x16, matrix products: 62.6 us -> 64 us  [the longest x1 13.8 us: local(): jnp.einsum('erd,efd->erf', grads_in, down_weight, preferred_element_type=...]
  transfers between devices with their start and end apart: 4 -> 4, of which waited for: 3 -> 4; matrix products, arithmetic and copies ran while one was open for 15% -> 16% of each run, Pallas kernels for 0% -> 0%
where the time goes in v1:
time: 442 us; the launch traced here: 437 us
  waiting for transfers between devices  289 us (65%)
  matrix products  64 us (14%)
  local copies, waits for them, and re-layouts  59.7 us (14%)
  starting transfers between devices  19.4 us (4%)
    all_to_all x4, waiting for transfers between devices, exchange(): return lax.all_to_all(value, 'ep', split_axis=0, concat_axis=0, tiled=True)  289 us
    all_to_all x4, local copies, waits for them, and re-layouts, exchange(): return lax.all_to_all(value, 'ep', split_axis=0, concat_axis=0, tiled=True)  24.6 us
    transpose x2, local copies, waits for them, and re-layouts, by_expert(): value.transpose(1, 0, 2, 3).reshape(owned, count * cap, value.shape[3])  21 us
    all_to_all x4, starting transfers between devices, exchange(): return lax.all_to_all(value, 'ep', split_axis=0, concat_axis=0, tiled=True)  19.4 us
    dot_general x1, matrix products, local(): jnp.einsum('erd,efd->erf', grads_in, down_weight, preferred_element_type=...  13.8 us
    dot_general x7, matrix products, dot(): return jnp.dot(a, b, preferred_element_type=F32)  12.5 us
    dot_general x1, matrix products, local(): jnp.einsum('erd,edf->erf', inputs, gate_weight, preferred_element_type=F32)  11.7 us
    dot_general x1, matrix products, local(): jnp.einsum('erf,edf->erd', deltas, joined[:, :half], preferred_element_ty...  8.84 us
  transfers between devices with their start and end apart: 4, of which 4 were waited for; matrix products, arithmetic and copies ran while one was open for 16% of the time, Pallas kernels for 0%

profile of v1, /device:TPU:0, one launch (start us, length us, event | category | flops | bytes accessed | tf_op | source)
XLA Modules:
  0.0 437.2 jit_solution(14517417133161467791)
XLA Ops:
  2.0 3.8 convolution_convert_fusion
  5.8 7.4 %all-to-all-start.1 = ((bf16[32,40,2048]{2,1,0:T(8,128)(2,1)}), bf16[32,40,2048]{2,1,0:T(8,128)(2,1)}, u32[]{:S(2)}, u32[]{:S(2)}) async-start(bf16[32,40,2048]{2,1,0:T(8,128)(2,1)} %bitcast.34), calls=%async_computation.1 | async-start | bytes 10485760 | tf_op jit(solution)/shard_map/all_to_all | solution.py:43
  13.3 3.9 convolution_convert_fusion.1
  17.2 112.6 %all-to-all-done.1 = bf16[32,40,2048]{2,1,0:T(8,128)(2,1)} async-done(((bf16[32,40,2048]{2,1,0:T(8,128)(2,1)}), bf16[32,40,2048]{2,1,0:T(8,128)(2,1)}, u32[]{:S(2)}, u32[]{:S(2)}) %all-to-all-start.1) | async-done | bytes 5242912 | tf_op jit(solution)/shard_map/all_to_all | solution.py:43
  129.8 3.9 all-to-all-start
  133.7 3.4 constant_dynamic-update-slice_fusion.1
  139.8 11.5 %copy.63 = bf16[32,40,2048]{2,0,1:T(8,128)(2,1)} copy(bf16[32,40,2048]{2,1,0:T(8,128)(2,1)} %all-to-all-done.1) | data formatting | bytes 10485760 | tf_op jit(solution)/shard_map/all_to_all | solution.py:43
  151.3 10.4 %copy.64 = bf16[2,32,20,2048]{3,0,2,1:T(2,128)(2,1)} copy(bf16[2,32,20,2048]{3,1,2,0:T(8,128)(2,1)} %bitcast.35) | data formatting | bytes 10485760 | tf_op jit(solution)/shard_map/transpose | solution.py:47
  161.7 11.7 %fusion.6 = f32[2,640,768]{2,1,0:T(8,128)} fusion(bf16[2,2048,768]{2,1,0:T(8,128)(2,1)} %param.11, bf16[2,640,2048]{2,0,1:T(2,128)(2,1)} %bitcast.46), kind=kOutput, calls=%fused_computation.8 | convolution fusion | flops 4026531840 | bytes 15466496 | tf_op jit(solution)/shard_map/erd,edf->erf/dot_general | solution.py:55
  173.4 7.2 %fusion.8 = f32[2,640,768]{2,1,0:T(8,128)} fusion(bf16[2,2048,768]{2,1,0:T(8,128)(2,1)S(1)} %bitcast.44, bf16[2,640,2048]{2,0,1:T(2,128)(2,1)S(1)} %bitcast.47), kind=kOutput, calls=%fused_computation.10 | convolution fusion | flops 4026531840 | bytes 15466496 | tf_op jit(solution)/shard_map/erd,edf->erf/dot_general | solution.py:56
  180.7 69.5 %all-to-all-done = bf16[32,40,2048]{2,1,0:T(8,128)(2,1)} async-done(((bf16[32,40,2048]{2,1,0:T(8,128)(2,1)}), bf16[32,40,2048]{2,1,0:T(8,128)(2,1)}, u32[]{:S(2)}, u32[]{:S(2)}) %all-to-all-start) | async-done | bytes 5242912 | tf_op jit(solution)/shard_map/all_to_all | solution.py:43
  250.1 7.7 %copy.60 = bf16[32,40,2048]{2,0,1:T(8,128)(2,1)} copy(bf16[32,40,2048]{2,1,0:T(8,128)(2,1)} %all-to-all-done) | data formatting | bytes 10485760 | tf_op jit(solution)/shard_map/all_to_all | solution.py:43
  257.8 10.6 %copy.61 = bf16[2,32,20,2048]{3,0,2,1:T(2,128)(2,1)} copy(bf16[2,32,20,2048]{3,1,2,0:T(8,128)(2,1)} %bitcast.36) | data formatting | bytes 10485760 | tf_op jit(solution)/shard_map/transpose | solution.py:47
  268.4 13.8 %multiply_reduce_fusion = (f32[2,640]{1,0:T(2,128)S(1)}, bf16[2,640,768]{2,1,0:T(8,128)(2,1)S(1)}, bf16[2,640,768]{2,1,0:T(8,128)(2,1)S(1)}) fusion(f32[2,640,768]{2,1,0:T(8,128)} %fusion.8, f32[2,640,768]{2,1,0:T(8,128)} %fusion.6, bf16[2,768,2048]{2,1,0:T(8,128)(2,1)} %param.13, bf16[2,640,2048]{2,0,1:T(2,128)(2,1)} %bitcast.45), kind=kOutput, calls=%fused_computation.13 | convolution fusion | flops 4042259200 | bytes 23335936 | tf_op jit(solution)/shard_map/erd,efd->erf/dot_general | solution.py:57
  282.2 8.8 %fusion.15 = bf16[2,640,1024]{2,1,0:T(8,128)(2,1)S(1)} fusion(bf16[2,2048,1536]{2,1,0:T(8,128)(2,1)} %copy-done.3, bf16[2,640,768]{2,1,0:T(8,128)(2,1)S(1)} %get-tuple-element.8, bf16[2,640,768]{2,1,0:T(8,128)(2,1)S(1)} %get-tuple-element.7), kind=kOutput, calls=%fused_computation.27 | convolution fusion | flops 4035706880 | bytes 12845056 | tf_op jit(solution)/shard_map/erf,edf->erd/dot_general | solution.py:70
  291.8 3.0 copy.67
  297.7 3.7 all-to-all-start.2
  301.5 8.2 %fusion.18 = bf16[2,640,1024]{2,1,0:T(8,128)(2,1)S(1)} fusion(bf16[2,2048,1536]{2,1,0:T(8,128)(2,1)} %copy-done.3, bf16[2,640,768]{2,1,0:T(8,128)(2,1)} %copy-done.12, bf16[2,640,768]{2,1,0:T(8,128)(2,1)} %copy-done.11), kind=kOutput, calls=%fused_computation.28 | convolution fusion | flops 4035706880 | bytes 12845056 | tf_op jit(solution)/shard_map/erf,edf->erd/dot_general | solution.py:71
  309.7 2.7 copy.70
  313.8 2.9 copy.72
  316.8 51.8 %all-to-all-done.2 = bf16[32,40,1152]{2,1,0:T(8,128)(2,1)S(1)} async-done(((bf16[32,40,1152]{2,1,0:T(8,128)(2,1)}), bf16[32,40,1152]{2,1,0:T(8,128)(2,1)S(1)}, u32[]{:S(2)}, u32[]{:S(2)}) %all-to-all-start.2) | async-done | bytes 2949152 | tf_op jit(solution)/shard_map/all_to_all | solution.py:43
  368.6 4.4 all-to-all-start.3
  377.4 55.6 %all-to-all-done.3 = bf16[32,40,1024]{2,1,0:T(8,128)(2,1)} async-done(((bf16[32,40,1024]{2,1,0:T(8,128)(2,1)}), bf16[32,40,1024]{2,1,0:T(8,128)(2,1)}, u32[]{:S(2)}, u32[]{:S(2)}) %all-to-all-start.3) | async-done | bytes 2621472 | tf_op jit(solution)/shard_map/all_to_all | solution.py:43
  433.0 2.8 fusion.23
  (60 shorter events, 14.5 us)
Async XLA Ops:
  0.6 1.4 copy-start
  1.6 4.3 copy-start.9
  5.8 7.5 %copy-start.4 = (bf16[128,2048]{1,0:T(8,128)(2,1)S(1)}, bf16[128,2048]{1,0:T(8,128)(2,1)}, u32[]{:S(2)}) copy-start(bf16[128,2048]{1,0:T(8,128)(2,1)} %param.8) | copy-start | bytes 1572868
  5.8 123.9 %all-to-all-start.1 = ((bf16[32,40,2048]{2,1,0:T(8,128)(2,1)}), bf16[32,40,2048]{2,1,0:T(8,128)(2,1)}, u32[]{:S(2)}, u32[]{:S(2)}) async-start(bf16[32,40,2048]{2,1,0:T(8,128)(2,1)} %bitcast.34), calls=%async_computation.1 | async-start | bytes 10485760 | tf_op jit(solution)/shard_map/all_to_all | solution.py:43
  129.8 120.4 %all-to-all-start = ((bf16[32,40,2048]{2,1,0:T(8,128)(2,1)}), bf16[32,40,2048]{2,1,0:T(8,128)(2,1)}, u32[]{:S(2)}, u32[]{:S(2)}) async-start(bf16[32,40,2048]{2,1,0:T(8,128)(2,1)} %bitcast.33), calls=%async_computation | async-start | bytes 10485760 | tf_op jit(solution)/shard_map/all_to_all | solution.py:43
  133.7 4.0 slice-start
  133.7 4.7 %slice-start.1 = ((s8[6291456]{0:T(1024)(128)(4,1)}), s8[2097152]{0:T(1024)(128)(4,1)S(1)}, s32[]{:S(2)}) async-start(s8[6291456]{0:T(1024)(128)(4,1)} %bitcast.41), calls=%async_computation.5 | async-start | bytes 4194304
  139.8 11.5 %copy-start.3 = (bf16[2,2048,1536]{2,1,0:T(8,128)(2,1)}, bf16[2,2048,1536]{2,1,0:T(8,128)(2,1)S(1)}, u32[]{:S(2)}) copy-start(bf16[2,2048,1536]{2,1,0:T(8,128)(2,1)S(1)} %constant_dynamic-update-slice_fusion) | copy-start | bytes 37748740
  151.3 22.1 %slice-start.2 = ((s8[6291456]{0:T(1024)(128)(4,1)}), s8[2097152]{0:T(1024)(128)(4,1)S(1)}, s32[]{:S(2)}) async-start(s8[6291456]{0:T(1024)(128)(4,1)} %bitcast.43), calls=%async_computation.6 | async-start | bytes 4194304
  161.7 11.7 %slice-start.3 = ((s8[6291456]{0:T(1024)(128)(4,1)}), s8[4194304]{0:T(1024)(128)(4,1)S(1)}, s32[]{:S(2)}) async-start(s8[6291456]{0:T(1024)(128)(4,1)} %bitcast.43), calls=%async_computation.7 | async-start | bytes 8388608
  161.7 11.7 %copy-start.2 = (bf16[2,32,20,2048]{3,0,2,1:T(2,128)(2,1)S(1)}, bf16[2,32,20,2048]{3,0,2,1:T(2,128)(2,1)}, u32[]{:S(2)}) copy-start(bf16[2,32,20,2048]{3,0,2,1:T(2,128)(2,1)} %copy.64) | copy-start | bytes 15728644
  282.2 8.9 %copy-start.11 = (bf16[2,640,768]{2,1,0:T(8,128)(2,1)}, bf16[2,640,768]{2,1,0:T(8,128)(2,1)S(1)}, u32[]{:S(2)}) copy-start(bf16[2,640,768]{2,1,0:T(8,128)(2,1)S(1)} %get-tuple-element.7) | copy-start | bytes 5898244
  282.2 8.9 %copy-start.12 = (bf16[2,640,768]{2,1,0:T(8,128)(2,1)}, bf16[2,640,768]{2,1,0:T(8,128)(2,1)S(1)}, u32[]{:S(2)}) copy-start(bf16[2,640,768]{2,1,0:T(8,128)(2,1)S(1)} %get-tuple-element.8) | copy-start | bytes 5898244
  297.7 70.9 %all-to-all-start.2 = ((bf16[32,40,1152]{2,1,0:T(8,128)(2,1)}), bf16[32,40,1152]{2,1,0:T(8,128)(2,1)S(1)}, u32[]{:S(2)}, u32[]{:S(2)}) async-start(bf16[32,40,1152]{2,1,0:T(8,128)(2,1)} %copy.69), calls=%async_computation.2 | async-start | bytes 5898240 | tf_op jit(solution)/shard_map/all_to_all | solution.py:43
  316.8 56.2 %copy-start.10 = (bf16[128,64]{0,1:T(8,128)(2,1)S(1)}, bf16[128,64]{0,1:T(8,128)(2,1)}, u32[]{:S(2)}) copy-start(bf16[128,64]{0,1:T(8,128)(2,1)} %copy-done.9) | copy-start | bytes 49156
  316.8 58.1 %copy-start.5 = (s32[128,8]{0,1:T(8,128)S(1)}, s32[128,8]{0,1:T(8,128)}, u32[]{:S(2)}) copy-start(s32[128,8]{0,1:T(8,128)} %param.10) | copy-start | bytes 12292
  316.8 58.1 %copy-start.6 = (f32[128,8]{0,1:T(8,128)S(1)}, f32[128,8]{0,1:T(8,128)}, u32[]{:S(2)}) copy-start(f32[128,8]{0,1:T(8,128)} %param.9) | copy-start | bytes 12292
  368.6 64.4 %all-to-all-start.3 = ((bf16[32,40,1024]{2,1,0:T(8,128)(2,1)}), bf16[32,40,1024]{2,1,0:T(8,128)(2,1)}, u32[]{:S(2)}, u32[]{:S(2)}) async-start(bf16[32,40,1024]{2,1,0:T(8,128)(2,1)} %copy.72), calls=%async_computation.3 | async-start | bytes 5242880 | tf_op jit(solution)/shard_map/all_to_all | solution.py:43
  376.0 1.4 copy-start.7
  376.5 0.9 copy-start.8
  433.0 4.0 copy-start.1
